TPU v7x, 32 devices: a whole 2x2x4 slice. The times are simulated.
32 devices in a mesh: grp: 4 (over y, x), tp: 8 (over z, core).
Axes of the slice: x: 2, y: 2, z: 4, core: 2. Of those that a mesh axis runs over, the one named last changes fastest.
Arguments:
- teacher_in: bfloat16 [192, 8192], P('tp', 'grp'), may hold values from -6 to 6
- teacher_gate: bfloat16 [8192, 28672], P('grp', 'tp'), may hold values from -0.0625 to 0.0625
- teacher_up: bfloat16 [8192, 28672], P('grp', 'tp'), may hold values from -0.0625 to 0.0625
- teacher_down: bfloat16 [28672, 8192], P('tp', 'grp'), may hold values from -0.046875 to 0.046875
- student_in: bfloat16 [192, 4096], P('tp', 'grp'), may hold values from -6 to 6
- student_gate: bfloat16 [4096, 14336], P('grp', 'tp'), may hold values from -0.09375 to 0.09375
- student_up: bfloat16 [4096, 14336], P('grp', 'tp'), may hold values from -0.09375 to 0.09375
- student_down: bfloat16 [14336, 4096], P('tp', 'grp'), may hold values from -0.046875 to 0.046875
- projector: bfloat16 [4096, 4, 2048], P('grp', None, 'tp'), may hold values from -0.09375 to 0.09375
Outputs:
- grad_input: float32 [192, 4096], P('tp', 'grp')
- grad_gate: float32 [4096, 14336], P('grp', 'tp')
- grad_up: float32 [4096, 14336], P('grp', 'tp')
- grad_down: float32 [14336, 4096], P('tp', 'grp')
- grad_projector: float32 [4096, 4, 2048], P('grp', None, 'tp')
All inputs are finite; a program needn't handle non-finite values.
Results may differ from a plain program's by a relative error of at most 0.017.
Values may be sent and summed in bfloat16 or wider, within the bound.
No kernel may reach another device: no remote copies, remote signals or barrier semaphores. Data moves between devices by JAX's collectives and lax.ppermute only.
A program may use at most 192 MiB of HBM per device.

v0:
```python
import jax
import jax.numpy as jnp
from jax import lax
from jax.sharding import PartitionSpec as P


def body(
    teacher_in,
    teacher_gate,
    teacher_up,
    teacher_down,
    student_in,
    student_gate,
    student_up,
    student_down,
    projector,
):
    bf = jnp.bfloat16
    fl = jnp.float32
    teacher_pair = jnp.concatenate([teacher_gate, teacher_up], axis=1)
    teacher_width = teacher_gate.shape[1]
    teacher_partial = jnp.dot(
        lax.all_gather(teacher_in, "tp", axis=0, tiled=True),
        teacher_pair,
        preferred_element_type=fl,
    )
    teacher_pre = lax.psum_scatter(teacher_partial, "grp", scatter_dimension=0, tiled=True)
    teacher_hidden = (
        jax.nn.silu(teacher_pre[:, :teacher_width]) * teacher_pre[:, teacher_width:]
    ).astype(bf)
    teacher_sums = jnp.dot(
        lax.all_gather(teacher_hidden, "grp", axis=0, tiled=True),
        teacher_down,
        preferred_element_type=fl,
    )
    teacher_share = lax.psum_scatter(teacher_sums, "tp", scatter_dimension=1, tiled=True)
    teacher_feature = lax.all_to_all(
        teacher_share.astype(bf), "grp", split_axis=0, concat_axis=1, tiled=True
    )
    student_pair = jnp.concatenate([student_gate, student_up], axis=1)
    student_width = student_gate.shape[1]
    input_rows = lax.all_gather(student_in, "tp", axis=0, tiled=True)
    student_partial = jnp.dot(input_rows, student_pair, preferred_element_type=fl)
    student_pre = lax.psum_scatter(student_partial, "grp", scatter_dimension=0, tiled=True)
    gate_values = student_pre[:, :student_width]
    up_values = student_pre[:, student_width:]
    student_hidden = (jax.nn.silu(gate_values) * up_values).astype(bf)
    hidden_rows = lax.all_gather(student_hidden, "grp", axis=0, tiled=True)
    feature_sum = lax.psum(jnp.dot(hidden_rows, student_down, preferred_element_type=fl), "tp")
    student_feature = feature_sum.astype(bf)
    proj_matrix = projector.reshape(projector.shape[0], -1)
    projected = lax.psum_scatter(
        jnp.dot(student_feature, proj_matrix, preferred_element_type=fl),
        "grp",
        scatter_dimension=0,
        tiled=True,
    )
    residual_grad = (projected - teacher_feature.astype(fl)).astype(bf)
    residual_rows = lax.all_gather(residual_grad, "grp", axis=0, tiled=True)
    grad_projector = jnp.dot(student_feature.T, residual_rows, preferred_element_type=fl).reshape(
        projector.shape
    )
    feature_grad = lax.psum(
        jnp.dot(residual_rows, proj_matrix.T, preferred_element_type=fl), "tp"
    ).astype(bf)
    grad_down = jnp.dot(hidden_rows.T, feature_grad, preferred_element_type=fl)
    hidden_grad = lax.psum_scatter(
        jnp.dot(feature_grad, student_down.T, preferred_element_type=fl),
        "grp",
        scatter_dimension=0,
        tiled=True,
    )
    sigmoid_gate = jax.nn.sigmoid(gate_values)
    gate_grad = (
        hidden_grad * up_values * sigmoid_gate * (1.0 + gate_values * (1.0 - sigmoid_gate))
    ).astype(bf)
    up_grad = (hidden_grad * gate_values * sigmoid_gate).astype(bf)
    pair_rows = lax.all_gather(
        jnp.concatenate([gate_grad, up_grad], axis=1), "grp", axis=0, tiled=True
    )
    grad_pair = jnp.dot(input_rows.T, pair_rows, preferred_element_type=fl)
    grad_input = lax.psum_scatter(
        jnp.dot(pair_rows, student_pair.T, preferred_element_type=fl).astype(jnp.bfloat16),
        "tp",
        scatter_dimension=0,
        tiled=True,
    ).astype(jnp.float32)
    return (
        grad_input,
        grad_pair[:, :student_width],
        grad_pair[:, student_width:],
        grad_down,
        grad_projector,
    )


def solution(mesh):
    placed = (
        P("tp", "grp"),
        P("grp", "tp"),
        P("grp", "tp"),
        P("tp", "grp"),
        P("tp", "grp"),
        P("grp", "tp"),
        P("grp", "tp"),
        P("tp", "grp"),
        P("grp", None, "tp"),
    )
    return jax.shard_map(
        body,
        mesh=mesh,
        in_specs=placed,
        out_specs=(
            P("tp", "grp"),
            P("grp", "tp"),
            P("grp", "tp"),
            P("tp", "grp"),
            P("grp", None, "tp"),
        ),
        check_vma=False,
    )
```

profile of v0, /device:TPU:0, one launch (start us, length us, event | category | flops | bytes accessed | tf_op | source)
XLA Modules:
  0.0 422.7 jit_solution(930207206825908747)
XLA Ops:
  7.2 17.4 %all_gather.20 = bf16[192,2048]{1,0:T(8,128)(2,1)S(1)} all-gather(bf16[24,2048]{1,0:T(8,128)(2,1)} %param.9), channel_id=1, replica_groups=mesh['grp'=4,'tp'=8] {'tp'}, dimensions={0}, use_global_device_ids=true | all-gather | bytes 884736 | tf_op jit(solution)/shard_map/all_gather | solution.py:23
  24.6 14.3 %fusion.4 = f32[192,7168]{1,0:T(8,128)} fusion(bf16[192,2048]{1,0:T(8,128)(2,1)S(1)} %all_gather.20, bf16[2048,3584]{1,0:T(8,128)(2,1)} %param.11, bf16[2048,3584]{1,0:T(8,128)(2,1)} %param.10), kind=kOutput, calls=%fused_computation.4 | convolution fusion | flops 5695864832 | bytes 35651584 | tf_op jit(solution)/shard_map/dot_general | solution.py:22
  39.0 64.8 %reduce-scatter.11.cloned.1.call-done = f32[48,7168]{1,0:T(8,128)} async-done(((f32[192,7168]{1,0:T(8,128)}), f32[48,7168]{1,0:T(8,128)}) %reduce-scatter.11.cloned.1.call-update) | async-done | bytes 1376272 | tf_op jit(solution)/shard_map/reduce_scatter | solution.py:27
  106.1 14.6 %all_gather.18 = bf16[192,1024]{1,0:T(8,128)(2,1)S(1)} all-gather(bf16[24,1024]{1,0:T(8,128)(2,1)S(1)} %copy-done.8), channel_id=1, replica_groups=mesh['grp'=4,'tp'=8] {'tp'}, dimensions={0}, use_global_device_ids=true | all-gather | bytes 442368 | tf_op jit(solution)/shard_map/all_gather | solution.py:42
  129.8 5.7 %all-gather.3.cloned.1.call-done = bf16[192,3584]{1,0:T(8,128)(2,1)} async-done(((bf16[48,3584]{1,0:T(8,128)(2,1)}), bf16[192,3584]{1,0:T(8,128)(2,1)}) %all-gather.3.cloned.1.call-update) | async-done | bytes 1376272 | tf_op jit(solution)/shard_map/all_gather | solution.py:32
  135.4 9.8 %fusion.19 = f32[192,2048]{1,0:T(8,128)} fusion(bf16[192,3584]{1,0:T(8,128)(2,1)} %all-gather.3.cloned.1.call-done, bf16[3584,2048]{1,0:T(8,128)(2,1)} %param.12), kind=kOutput, calls=%fused_computation.30 | convolution fusion | flops 2818572288 | bytes 17629184 | tf_op jit(solution)/shard_map/dot_general | solution.py:31
  147.4 32.3 %reduce-scatter.7.cloned.1.call-done = f32[48,3584]{1,0:T(8,128)} async-done(((f32[192,3584]{1,0:T(8,128)}), f32[48,3584]{1,0:T(8,128)}) %reduce-scatter.7.cloned.1.call-update) | async-done | bytes 688144 | tf_op jit(solution)/shard_map/reduce_scatter | solution.py:44
  180.9 10.7 %all_gather.19 = bf16[192,1792]{1,0:T(8,128)(2,1)S(1)} all-gather(bf16[48,1792]{1,0:T(8,128)(2,1)S(1)} %multiply_convert_fusion.2), channel_id=1, replica_groups=mesh['grp'=4,'tp'=8] {'grp'}, dimensions={0}, use_global_device_ids=true | all-gather | bytes 860160 | tf_op jit(solution)/shard_map/all_gather | solution.py:48
  191.6 3.8 fusion.18
  195.4 38.1 %all-reduce.2 = bf16[192,1024]{1,0:T(8,128)(2,1)S(1)} all-reduce(f32[192,1024]{1,0:T(8,128)} %fusion.18), channel_id=1, replica_groups=mesh['grp'=4,'tp'=8] {'tp'}, use_global_device_ids=true, to_apply=%region_1.2 | all-reduce | flops 196608 | bytes 1179648 | tf_op jit(solution)/shard_map/psum | solution.py:49
  236.1 7.8 %all_to_all.13 = bf16[4,48,256]{2,1,0:T(8,128)(2,1)S(1)} all-to-all(bf16[4,48,256]{2,1,0:T(8,128)(2,1)S(1)} %bitcast.40), channel_id=1, replica_groups=mesh['grp'=4,'tp'=8] {'grp'}, dimensions={0} | all-to-all | bytes 196608 | tf_op jit(solution)/shard_map/all_to_all | solution.py:37
  243.9 14.5 %reduce-scatter.9.cloned.1.call-done = f32[48,1024]{1,0:T(8,128)} async-done(((f32[192,1024]{1,0:T(8,128)}), f32[48,1024]{1,0:T(8,128)}) %reduce-scatter.9.cloned.1.call-update) | async-done | bytes 196624 | tf_op jit(solution)/shard_map/reduce_scatter | solution.py:52
  259.4 9.6 %all_gather.22 = bf16[192,1024]{1,0:T(8,128)(2,1)S(1)} all-gather(bf16[48,1024]{1,0:T(8,128)(2,1)S(1)} %subtract_convert_fusion), channel_id=1, replica_groups=mesh['grp'=4,'tp'=8] {'grp'}, dimensions={0}, use_global_device_ids=true | all-gather | bytes 491520 | tf_op jit(solution)/shard_map/all_gather | solution.py:59
  271.4 35.0 %all-reduce.3 = bf16[192,1024]{1,0:T(8,128)(2,1)S(1)} all-reduce(f32[192,1024]{1,0:T(8,128)} %fusion.20), channel_id=1, replica_groups=mesh['grp'=4,'tp'=8] {'tp'}, use_global_device_ids=true, to_apply=%region_5.6 | all-reduce | flops 196608 | bytes 1179648 | tf_op jit(solution)/shard_map/psum | solution.py:63
  306.4 4.5 %fusion.22 = f32[192,1792]{1,0:T(8,128)} fusion(bf16[192,1024]{1,0:T(8,128)(2,1)S(1)} %all-reduce.3, bf16[1792,1024]{1,0:T(8,128)(2,1)} %param.16), kind=kOutput, calls=%fused_computation.33 | convolution fusion | flops 704643072 | bytes 5439488 | tf_op jit(solution)/shard_map/dot_general | solution.py:68
  311.1 27.0 %reduce-scatter.15.cloned.1.call-done = f32[48,1792]{1,0:T(8,128)} async-done(((f32[192,1792]{1,0:T(8,128)}), f32[48,1792]{1,0:T(8,128)}) %reduce-scatter.15.cloned.1.call-update) | async-done | bytes 344080 | tf_op jit(solution)/shard_map/reduce_scatter | solution.py:67
  342.9 5.3 %copy.21 = f32[1024,4,256]{2,1,0:T(4,128)} copy(f32[1024,4,256]{0,2,1:T(8,128)} %bitcast.35) | data formatting | bytes 8388608
  348.2 4.2 fusion.21
  352.4 17.1 %all-gather.5.cloned.1.call-done = bf16[192,3584]{1,0:T(8,128)(2,1)} async-done(((bf16[48,3584]{1,0:T(8,128)(2,1)}), bf16[192,3584]{1,0:T(8,128)(2,1)}) %all-gather.5.cloned.1.call-update) | async-done | bytes 1376272 | tf_op jit(solution)/shard_map/all_gather | solution.py:78
  369.4 6.9 %convolution_convert_fusion = bf16[192,1024]{1,0:T(8,128)(2,1)} fusion(bf16[192,3584]{1,0:T(8,128)(2,1)} %all-gather.5.cloned.1.call-done, bf16[1024,3584]{1,0:T(8,128)(2,1)} %copy-done), kind=kOutput, calls=%fused_computation.7 | convolution fusion | flops 1409482752 | bytes 9109504 | tf_op jit(solution)/shard_map/dot_general | solution.py:83
  376.4 7.3 %convolution_bitcast_fusion = f32[1024,3584]{0,1:T(8,128)} fusion(bf16[192,3584]{1,0:T(8,128)(2,1)S(1)} %copy-done.7, bf16[192,1024]{1,0:T(8,128)(2,1)S(1)} %copy-done.2), kind=kOutput, calls=%fused_computation.5 | convolution fusion | flops 1409286144 | bytes 16449536 | tf_op jit(solution)/shard_map/dot_general | solution.py:81
  383.7 13.9 %fusion.17 = (f32[1024,1792]{0,1:T(8,128)}, f32[1024,1792]{0,1:T(8,128)}) fusion(f32[1024,3584]{0,1:T(8,128)} %convolution_bitcast_fusion), kind=kLoop, calls=%fused_computation.28 | loop fusion | bytes 29360128 | tf_op jit(solution)/shard_map/slice | solution.py:91
  397.6 8.4 %copy.19 = f32[1024,1792]{1,0:T(8,128)} copy(f32[1024,1792]{0,1:T(8,128)} %get-tuple-element.16) | data formatting | bytes 14680064
  406.0 8.4 %copy.20 = f32[1024,1792]{1,0:T(8,128)} copy(f32[1024,1792]{0,1:T(8,128)} %get-tuple-element.15) | data formatting | bytes 14680064
  (52 shorter events, 27.2 us)
Async XLA Ops:
  7.2 96.6 %reduce-scatter.11.cloned.1.call-start = ((), (), s32[]{:S(2)}) async-start(), calls=%async_computation.9 | async-start | bytes 6881280 | tf_op jit(solution)/shard_map/reduce_scatter | solution.py:27
  38.9 67.1 %copy-start.8 = (bf16[24,1024]{1,0:T(8,128)(2,1)S(1)}, bf16[24,1024]{1,0:T(8,128)(2,1)}, u32[]{:S(2)}) copy-start(bf16[24,1024]{1,0:T(8,128)(2,1)} %param.13) | copy-start | bytes 147460
  39.0 96.5 %all-gather.3.cloned.1.call-start = ((), (), s32[]{:S(2)}) async-start(), calls=%async_computation.10 | async-start | bytes 1720320 | tf_op jit(solution)/shard_map/all_gather | solution.py:32
  106.0 73.7 %reduce-scatter.7.cloned.1.call-start = ((), (), s32[]{:S(2)}) async-start(), calls=%async_computation.7 | async-start | bytes 3440640 | tf_op jit(solution)/shard_map/reduce_scatter | solution.py:44
  106.1 17.1 %copy-start.3 = (bf16[1024,1792]{1,0:T(8,128)(2,1)S(1)}, bf16[1024,1792]{1,0:T(8,128)(2,1)}, u32[]{:S(2)}) copy-start(bf16[1024,1792]{1,0:T(8,128)(2,1)} %param.15) | copy-start | bytes 11010052
  120.7 2.8 copy-start.1
  123.5 3.1 copy-start
  129.7 105.4 %reduce-scatter.13.cloned.1.call-start = ((), (), s32[]{:S(2)}) async-start(), calls=%async_computation.11 | async-start | bytes 1769472 | tf_op jit(solution)/shard_map/reduce_scatter | solution.py:36
  145.2 113.2 %reduce-scatter.9.cloned.1.call-start = ((), (), s32[]{:S(2)}) async-start(), calls=%async_computation.8 | async-start | bytes 983040 | tf_op jit(solution)/shard_map/reduce_scatter | solution.py:52
  235.0 103.1 %reduce-scatter.15.cloned.1.call-start = ((), (), s32[]{:S(2)}) async-start(), calls=%async_computation.12 | async-start | bytes 1720320 | tf_op jit(solution)/shard_map/reduce_scatter | solution.py:67
  268.9 0.7 copy-start.4
  271.4 66.8 %copy-start.6 = (f32[48,3584]{1,0:T(8,128)S(1)}, f32[48,3584]{1,0:T(8,128)}, u32[]{:S(2)}) copy-start(f32[48,3584]{1,0:T(8,128)} %reduce-scatter.7.cloned.1.call-done) | copy-start | bytes 2064388
  271.4 68.7 %copy-start.5 = (bf16[192,1024]{1,0:T(8,128)(2,1)S(1)}, bf16[192,1024]{1,0:T(8,128)(2,1)}, u32[]{:S(2)}) copy-start(bf16[192,1024]{1,0:T(8,128)(2,1)} %copy-done.4) | copy-start | bytes 1179652
  310.9 58.5 %all-gather.5.cloned.1.call-start = ((), (), s32[]{:S(2)}) async-start(), calls=%async_computation.13 | async-start | bytes 1720320 | tf_op jit(solution)/shard_map/all_gather | solution.py:78
  340.1 74.3 %reduce-scatter.17.cloned.1.call-start = ((), (), s32[]{:S(2)}) async-start(), calls=%async_computation.14 | async-start | bytes 442368 | tf_op jit(solution)/shard_map/reduce_scatter | solution.py:82
  352.4 24.0 %copy-start.2 = (bf16[192,1024]{1,0:T(8,128)(2,1)S(1)}, bf16[192,1024]{1,0:T(8,128)(2,1)}, u32[]{:S(2)}) copy-start(bf16[192,1024]{1,0:T(8,128)(2,1)} %copy-done.1) | copy-start | bytes 1179652
  369.4 6.9 %copy-start.7 = (bf16[192,3584]{1,0:T(8,128)(2,1)S(1)}, bf16[192,3584]{1,0:T(8,128)(2,1)}, u32[]{:S(2)}) copy-start(bf16[192,3584]{1,0:T(8,128)(2,1)} %all-gather.5.cloned.1.call-done) | copy-start | bytes 4128772
Sparse Core Ops, SparseCore 0:
  39.1 64.6 reduce-scatter.10
  106.2 29.1 all-gather.2
  139.0 40.6 reduce-scatter.6
  182.4 36.0 reduce-scatter.12
  235.2 23.2 reduce-scatter.8
  311.0 27.0 reduce-scatter.14
  340.2 29.1 all-gather.4
  376.5 31.1 reduce-scatter.16
where the time goes:
time: 424 us; the launch traced here: 423 us
  waiting for transfers between devices  161 us (38%)
  blocking collectives  133 us (31%)
  matrix products  59.9 us (14%)
  local copies, waits for them, and re-layouts  44.7 us (11%)
  between operations  14.3 us (3%)
  other arithmetic  8.64 us (2%)
    reduce_scatter x1, waiting for transfers between devices, body(): lax.psum_scatter(teacher_partial, 'grp', scatter_dimension=0, tiled=True)  64.8 us
    psum x1, blocking collectives, body(): lax.psum(jnp.dot(hidden_rows, student_down, preferred_element_type=fl), '...  38.1 us
    psum x1, blocking collectives, body(): lax.psum(jnp.dot(residual_rows, proj_matrix.T, preferred_element_type=fl)...  35 us
    reduce_scatter x1, waiting for transfers between devices, body(): lax.psum_scatter(student_partial, 'grp', scatter_dimension=0, tiled=True)  32.3 us
    unnamed x23, local copies, waits for them, and re-layouts  30.4 us
    reduce_scatter x1, waiting for transfers between devices, body(): lax.psum_scatter(jnp.dot(feature_grad, student_down.T, preferred_element_...  27 us
    all_gather x1, blocking collectives, body(): lax.all_gather(teacher_in, 'tp', axis=0, tiled=True)  17.4 us
    all_gather x1, waiting for transfers between devices, body(): lax.all_gather(jnp.concatenate([gate_grad, up_grad], axis=1), 'grp', axis...  17.1 us
  transfers between devices with their start and end apart: 8, of which 6 were waited for; matrix products, arithmetic and copies ran while one was open for 18% of the time, Pallas kernels for 0%

commit v1 on v0

--- a/solution.py
+++ b/solution.py
@@ -46,7 +46,9 @@
     up_values = student_pre[:, student_width:]
     student_hidden = (jax.nn.silu(gate_values) * up_values).astype(bf)
     hidden_rows = lax.all_gather(student_hidden, "grp", axis=0, tiled=True)
-    feature_sum = lax.psum(jnp.dot(hidden_rows, student_down, preferred_element_type=fl), "tp")
+    part = jnp.dot(hidden_rows, student_down, preferred_element_type=fl)
+    shards = lax.all_gather(part, "tp")
+    feature_sum = jnp.sum(shards, axis=0)
     student_feature = feature_sum.astype(bf)
     proj_matrix = projector.reshape(projector.shape[0], -1)
     projected = lax.psum_scatter(

time: 424 us -> 474 us (1.12)
  waiting for transfers between devices: 161 us -> 246 us
  blocking collectives: 133 us -> 96 us
    all_gather x0 -> x1, waiting for transfers between devices: none -> 54.6 us  [body(): shards = lax.all_gather(part, 'tp')]
    psum x1 -> x0, blocking collectives: 38.1 us -> none  [body(): lax.psum(jnp.dot(hidden_rows, student_down, preferred_element_type=fl), '...]
    reduce_scatter x1, waiting for transfers between devices: 0.02 us -> 30.6 us  [body(): lax.psum_scatter(teacher_sums, 'tp', scatter_dimension=1, tiled=True)]
    reduce_scatter x1, waiting for transfers between devices: 64.8 us -> 40.4 us  [body(): lax.psum_scatter(teacher_partial, 'grp', scatter_dimension=0, tiled=True)]
    reduce_scatter x1, waiting for transfers between devices: 32.3 us -> 41.9 us  [body(): lax.psum_scatter(student_partial, 'grp', scatter_dimension=0, tiled=True)]
    all_gather x1, waiting for transfers between devices: 5.65 us -> 15.3 us  [body(): lax.all_gather(teacher_hidden, 'grp', axis=0, tiled=True)]
  transfers between devices with their start and end apart: 8 -> 9, of which waited for: 6 -> 8; matrix products, arithmetic and copies ran while one was open for 18% -> 17% of each run, Pallas kernels for 0% -> 0%
where the time goes in v1:
time: 474 us; the launch traced here: 473 us
  waiting for transfers between devices  246 us (52%)
  blocking collectives  96 us (20%)
  matrix products  59.8 us (13%)
  local copies, waits for them, and re-layouts  45.6 us (10%)
  between operations  14 us (3%)
  other arithmetic  12.1 us (3%)
    all_gather x1, waiting for transfers between devices, body(): shards = lax.all_gather(part, 'tp')  54.6 us
    reduce_scatter x1, waiting for transfers between devices, body(): lax.psum_scatter(student_partial, 'grp', scatter_dimension=0, tiled=True)  41.9 us
    reduce_scatter x1, waiting for transfers between devices, body(): lax.psum_scatter(teacher_partial, 'grp', scatter_dimension=0, tiled=True)  40.4 us
    psum x1, blocking collectives, body(): lax.psum(jnp.dot(residual_rows, proj_matrix.T, preferred_element_type=fl)...  35.2 us
    unnamed x23, local copies, waits for them, and re-layouts  31.4 us
    reduce_scatter x1, waiting for transfers between devices, body(): lax.psum_scatter(teacher_sums, 'tp', scatter_dimension=1, tiled=True)  30.6 us
    reduce_scatter x1, waiting for transfers between devices, body(): lax.psum_scatter(jnp.dot(feature_grad, student_down.T, preferred_element_...  27.2 us
    reduce_scatter x1, waiting for transfers between devices, body(): lax.psum_scatter(jnp.dot(student_feature, proj_matrix, preferred_element_...  18.3 us
  transfers between devices with their start and end apart: 9, of which 8 were waited for; matrix products, arithmetic and copies ran while one was open for 17% of the time, Pallas kernels for 0%

profile of v1, /device:TPU:0, one launch (start us, length us, event | category | flops | bytes accessed | tf_op | source)
XLA Modules:
  0.0 473.4 jit_solution(17475646982938782250)
XLA Ops:
  7.2 17.4 %all_gather.28 = bf16[192,2048]{1,0:T(8,128)(2,1)S(1)} all-gather(bf16[24,2048]{1,0:T(8,128)(2,1)} %param.9), channel_id=1, replica_groups=mesh['grp'=4,'tp'=8] {'tp'}, dimensions={0}, use_global_device_ids=true | all-gather | bytes 884736 | tf_op jit(solution)/shard_map/all_gather | solution.py:23
  24.6 14.3 %fusion.4 = f32[192,7168]{1,0:T(8,128)} fusion(bf16[192,2048]{1,0:T(8,128)(2,1)S(1)} %all_gather.28, bf16[2048,3584]{1,0:T(8,128)(2,1)} %param.11, bf16[2048,3584]{1,0:T(8,128)(2,1)} %param.10), kind=kOutput, calls=%fused_computation.4 | convolution fusion | flops 5695864832 | bytes 35651584 | tf_op jit(solution)/shard_map/dot_general | solution.py:22
  39.7 14.6 %all_gather.24 = bf16[192,1024]{1,0:T(8,128)(2,1)S(1)} all-gather(bf16[24,1024]{1,0:T(8,128)(2,1)S(1)} %copy-done.8), channel_id=1, replica_groups=mesh['grp'=4,'tp'=8] {'tp'}, dimensions={0}, use_global_device_ids=true | all-gather | bytes 442368 | tf_op jit(solution)/shard_map/all_gather | solution.py:42
  63.4 40.4 %reduce-scatter.11.cloned.1.call-done = f32[48,7168]{1,0:T(8,128)} async-done(((f32[192,7168]{1,0:T(8,128)}), f32[48,7168]{1,0:T(8,128)}) %reduce-scatter.11.cloned.1.call-update) | async-done | bytes 1376272 | tf_op jit(solution)/shard_map/reduce_scatter | solution.py:27
  106.1 41.9 %reduce-scatter.7.cloned.1.call-done = f32[48,3584]{1,0:T(8,128)} async-done(((f32[192,3584]{1,0:T(8,128)}), f32[48,3584]{1,0:T(8,128)}) %reduce-scatter.7.cloned.1.call-update) | async-done | bytes 688144 | tf_op jit(solution)/shard_map/reduce_scatter | solution.py:44
  149.2 10.7 %all_gather.25 = bf16[192,1792]{1,0:T(8,128)(2,1)S(1)} all-gather(bf16[48,1792]{1,0:T(8,128)(2,1)S(1)} %multiply_convert_fusion.2), channel_id=1, replica_groups=mesh['grp'=4,'tp'=8] {'grp'}, dimensions={0}, use_global_device_ids=true | all-gather | bytes 860160 | tf_op jit(solution)/shard_map/all_gather | solution.py:48
  163.8 15.3 %all-gather.5.cloned.1.call-done = bf16[192,3584]{1,0:T(8,128)(2,1)} async-done(((bf16[48,3584]{1,0:T(8,128)(2,1)}), bf16[192,3584]{1,0:T(8,128)(2,1)}) %all-gather.5.cloned.1.call-update) | async-done | bytes 1376272 | tf_op jit(solution)/shard_map/all_gather | solution.py:32
  179.1 9.8 %fusion.19 = f32[192,2048]{1,0:T(8,128)} fusion(bf16[192,3584]{1,0:T(8,128)(2,1)} %all-gather.5.cloned.1.call-done, bf16[3584,2048]{1,0:T(8,128)(2,1)} %param.12), kind=kOutput, calls=%fused_computation.30 | convolution fusion | flops 2818572288 | bytes 17629184 | tf_op jit(solution)/shard_map/dot_general | solution.py:31
  191.3 54.6 %all-gather.9.cloned.1.call-done = f32[1536,1024]{1,0:T(8,128)} async-done(((f32[192,1024]{1,0:T(8,128)}), f32[1536,1024]{1,0:T(8,128)}) %all-gather.9.cloned.1.call-update) | async-done | bytes 6291472 | tf_op jit(solution)/shard_map/all_gather | solution.py:50
  250.9 30.6 %reduce-scatter.13.cloned.1.call-done = f32[192,256]{1,0:T(8,128)} async-done(((f32[192,2048]{1,0:T(8,128)}), f32[192,256]{1,0:T(8,128)}) %reduce-scatter.13.cloned.1.call-update) | async-done | bytes 196624 | tf_op jit(solution)/shard_map/reduce_scatter | solution.py:36
  282.5 8.5 %all_to_all.13 = bf16[4,48,256]{2,1,0:T(8,128)(2,1)S(1)} all-to-all(bf16[4,48,256]{2,1,0:T(8,128)(2,1)S(1)} %bitcast.42), channel_id=1, replica_groups=mesh['grp'=4,'tp'=8] {'grp'}, dimensions={0} | all-to-all | bytes 196608 | tf_op jit(solution)/shard_map/all_to_all | solution.py:37
  291.0 18.3 %reduce-scatter.9.cloned.1.call-done = f32[48,1024]{1,0:T(8,128)} async-done(((f32[192,1024]{1,0:T(8,128)}), f32[48,1024]{1,0:T(8,128)}) %reduce-scatter.9.cloned.1.call-update) | async-done | bytes 196624 | tf_op jit(solution)/shard_map/reduce_scatter | solution.py:54
  310.2 9.6 %all_gather.30 = bf16[192,1024]{1,0:T(8,128)(2,1)S(1)} all-gather(bf16[48,1024]{1,0:T(8,128)(2,1)S(1)} %subtract_convert_fusion), channel_id=1, replica_groups=mesh['grp'=4,'tp'=8] {'grp'}, dimensions={0}, use_global_device_ids=true | all-gather | bytes 491520 | tf_op jit(solution)/shard_map/all_gather | solution.py:61
  322.3 35.2 %all-reduce.1 = bf16[192,1024]{1,0:T(8,128)(2,1)S(1)} all-reduce(f32[192,1024]{1,0:T(8,128)} %fusion.20), channel_id=1, replica_groups=mesh['grp'=4,'tp'=8] {'tp'}, use_global_device_ids=true, to_apply=%region_5.6 | all-reduce | flops 196608 | bytes 1179648 | tf_op jit(solution)/shard_map/psum | solution.py:65
  357.5 4.5 fusion.22
  362.0 27.2 %reduce-scatter.15.cloned.1.call-done = f32[48,1792]{1,0:T(8,128)} async-done(((f32[192,1792]{1,0:T(8,128)}), f32[48,1792]{1,0:T(8,128)}) %reduce-scatter.15.cloned.1.call-update) | async-done | bytes 344080 | tf_op jit(solution)/shard_map/reduce_scatter | solution.py:69
  394.0 5.3 %copy.21 = f32[1024,4,256]{2,1,0:T(4,128)} copy(f32[1024,4,256]{0,2,1:T(8,128)} %bitcast.36) | data formatting | bytes 8388608
  399.2 4.2 fusion.21
  403.4 17.1 %all-gather.7.cloned.1.call-done = bf16[192,3584]{1,0:T(8,128)(2,1)} async-done(((bf16[48,3584]{1,0:T(8,128)(2,1)}), bf16[192,3584]{1,0:T(8,128)(2,1)}) %all-gather.7.cloned.1.call-update) | async-done | bytes 1376272 | tf_op jit(solution)/shard_map/all_gather | solution.py:80
  420.5 6.9 %convolution_convert_fusion = bf16[192,1024]{1,0:T(8,128)(2,1)} fusion(bf16[192,3584]{1,0:T(8,128)(2,1)} %all-gather.7.cloned.1.call-done, bf16[1024,3584]{1,0:T(8,128)(2,1)} %copy-done), kind=kOutput, calls=%fused_computation.7 | convolution fusion | flops 1409482752 | bytes 9109504 | tf_op jit(solution)/shard_map/dot_general | solution.py:85
  427.4 7.3 %convolution_bitcast_fusion = f32[1024,3584]{0,1:T(8,128)} fusion(bf16[192,3584]{1,0:T(8,128)(2,1)S(1)} %copy-done.7, bf16[192,1024]{1,0:T(8,128)(2,1)S(1)} %copy-done.2), kind=kOutput, calls=%fused_computation.5 | convolution fusion | flops 1409286144 | bytes 16449536 | tf_op jit(solution)/shard_map/dot_general | solution.py:83
  434.7 13.9 %fusion.17 = (f32[1024,1792]{0,1:T(8,128)}, f32[1024,1792]{0,1:T(8,128)}) fusion(f32[1024,3584]{0,1:T(8,128)} %convolution_bitcast_fusion), kind=kLoop, calls=%fused_computation.28 | loop fusion | bytes 29360128 | tf_op jit(solution)/shard_map/slice | solution.py:93
  448.7 8.4 %copy.19 = f32[1024,1792]{1,0:T(8,128)} copy(f32[1024,1792]{0,1:T(8,128)} %get-tuple-element.16) | data formatting | bytes 14680064
  457.0 8.4 %copy.20 = f32[1024,1792]{1,0:T(8,128)} copy(f32[1024,1792]{0,1:T(8,128)} %get-tuple-element.15) | data formatting | bytes 14680064
  (55 shorter events, 35.2 us)
Async XLA Ops:
  7.2 96.6 %reduce-scatter.11.cloned.1.call-start = ((), (), s32[]{:S(2)}) async-start(), calls=%async_computation.9 | async-start | bytes 6881280 | tf_op jit(solution)/shard_map/reduce_scatter | solution.py:27
  38.9 0.8 copy-start.8
  39.0 109.1 %reduce-scatter.7.cloned.1.call-start = ((), (), s32[]{:S(2)}) async-start(), calls=%async_computation.7 | async-start | bytes 3440640 | tf_op jit(solution)/shard_map/reduce_scatter | solution.py:44
  39.7 17.1 %copy-start.3 = (bf16[1024,1792]{1,0:T(8,128)(2,1)S(1)}, bf16[1024,1792]{1,0:T(8,128)(2,1)}, u32[]{:S(2)}) copy-start(bf16[1024,1792]{1,0:T(8,128)(2,1)} %param.15) | copy-start | bytes 11010052
  54.3 2.8 copy-start.1
  57.1 3.1 copy-start
  63.3 115.8 %all-gather.5.cloned.1.call-start = ((), (), s32[]{:S(2)}) async-start(), calls=%async_computation.10 | async-start | bytes 1720320 | tf_op jit(solution)/shard_map/all_gather | solution.py:32
  106.0 139.9 %all-gather.9.cloned.1.call-start = ((), (), s32[]{:S(2)}) async-start(), calls=%async_computation.15 | async-start | bytes 7077888 | tf_op jit(solution)/shard_map/all_gather | solution.py:50
  163.8 117.7 %reduce-scatter.13.cloned.1.call-start = ((), (), s32[]{:S(2)}) async-start(), calls=%async_computation.11 | async-start | bytes 1769472 | tf_op jit(solution)/shard_map/reduce_scatter | solution.py:36
  188.9 120.4 %reduce-scatter.9.cloned.1.call-start = ((), (), s32[]{:S(2)}) async-start(), calls=%async_computation.8 | async-start | bytes 983040 | tf_op jit(solution)/shard_map/reduce_scatter | solution.py:54
  250.9 138.3 %reduce-scatter.15.cloned.1.call-start = ((), (), s32[]{:S(2)}) async-start(), calls=%async_computation.12 | async-start | bytes 1720320 | tf_op jit(solution)/shard_map/reduce_scatter | solution.py:69
  319.8 0.7 copy-start.4
  322.3 66.9 %copy-start.6 = (f32[48,3584]{1,0:T(8,128)S(1)}, f32[48,3584]{1,0:T(8,128)}, u32[]{:S(2)}) copy-start(f32[48,3584]{1,0:T(8,128)} %reduce-scatter.7.cloned.1.call-done) | copy-start | bytes 2064388
  322.3 68.9 %copy-start.5 = (bf16[192,1024]{1,0:T(8,128)(2,1)S(1)}, bf16[192,1024]{1,0:T(8,128)(2,1)}, u32[]{:S(2)}) copy-start(bf16[192,1024]{1,0:T(8,128)(2,1)} %copy-done.4) | copy-start | bytes 1179652
  362.0 58.5 %all-gather.7.cloned.1.call-start = ((), (), s32[]{:S(2)}) async-start(), calls=%async_computation.13 | async-start | bytes 1720320 | tf_op jit(solution)/shard_map/all_gather | solution.py:80
  391.1 74.3 %reduce-scatter.17.cloned.1.call-start = ((), (), s32[]{:S(2)}) async-start(), calls=%async_computation.14 | async-start | bytes 442368 | tf_op jit(solution)/shard_map/reduce_scatter | solution.py:84
  403.4 24.0 %copy-start.2 = (bf16[192,1024]{1,0:T(8,128)(2,1)S(1)}, bf16[192,1024]{1,0:T(8,128)(2,1)}, u32[]{:S(2)}) copy-start(bf16[192,1024]{1,0:T(8,128)(2,1)} %copy-done.1) | copy-start | bytes 1179652
  420.5 6.9 %copy-start.7 = (bf16[192,3584]{1,0:T(8,128)(2,1)S(1)}, bf16[192,3584]{1,0:T(8,128)(2,1)}, u32[]{:S(2)}) copy-start(bf16[192,3584]{1,0:T(8,128)(2,1)} %all-gather.7.cloned.1.call-done) | copy-start | bytes 4128772
Sparse Core Ops, SparseCore 0:
  39.1 64.6 reduce-scatter.10
  107.4 40.6 reduce-scatter.6
  149.9 29.1 all-gather.4
  181.2 64.6 all-gather.8
  248.6 32.8 reduce-scatter.12
  284.8 24.3 reduce-scatter.8
  362.1 27.0 reduce-scatter.14
  391.3 29.1 all-gather.6
  427.5 31.0 reduce-scatter.16
